TPU v7x, 256 devices: a whole 4x4x8 slice. The times are simulated.
256 devices in a mesh: wide: 64 (over z, y, core), lev: 4 (over x).
Axes of the slice: x: 4, y: 4, z: 8, core: 2. Of those that a mesh axis runs over, the one named last changes fastest.
Arguments:
- spec_in: bfloat16 [320, 2, 4, 641], P('wide', None, 'lev'), may hold values from -0.0068359375 to 0.0068359375
- legendre: bfloat16 [320, 641, 1280], P('wide'), may hold values from -4 to 4
- wind: bfloat16 [1280, 4, 2560], P(('wide', 'lev')), may hold values from -6 to 6
- lat_weight: float32 [1280], replicated, may hold values from 1 to 4
- wave_order: int32 [640], replicated, may hold values from 0 to 639, as said below
- lat_order: int32 [1280], replicated, may hold values from 0 to 1279, each once
- active: int32 [1280], replicated, may hold values from 5 to 640, as said below
Outputs:
- grid: bfloat16 [1280, 4, 2560], P(('wide', 'lev'))
- spec_out: float32 [320, 2, 4, 641], P('wide', None, 'lev')
Inputs may be any that keep to these rules, and one draw needn't show every extreme that they name: `wave_order`: A permutation in which slots 2p and 2p + 1 hold wavenumbers m and 639 - m. `lat_order`: each latitude once. `active`: equals 640 at some latitudes of every draw.
All inputs are finite; a program needn't handle non-finite values.
Results may differ from a plain program's by a relative error of at most 0.0072.
Values may be sent and summed in bfloat16 or wider, within the bound.
No kernel may reach another device: no remote copies, remote signals or barrier semaphores. Data moves between devices by JAX's collectives and lax.ppermute only.
A program may use at most 64 MiB of HBM per device.

v0:
```python
import math
import jax
import jax.numpy as jnp
from jax import lax
from jax.sharding import PartitionSpec as P


def make_basis(wave_order, live_count, points):
    cell_count = 4 * live_count
    cell_float = cell_count.astype(jnp.float32)
    outer_count = points // 128
    outer_ids = jnp.arange(outer_count, dtype=jnp.int32) * 128
    inner_ids = jnp.arange(128, dtype=jnp.int32)
    outer_phase = wave_order[:, None] * outer_ids[None, :] % cell_count
    inner_phase = wave_order[:, None] * inner_ids[None, :] % cell_count
    outer_angle = outer_phase.astype(jnp.float32) * (2.0 * math.pi) / cell_float
    inner_angle = inner_phase.astype(jnp.float32) * (2.0 * math.pi) / cell_float
    cos_outer = jnp.cos(outer_angle)[:, :, None]
    sin_outer = jnp.sin(outer_angle)[:, :, None]
    cos_inner = jnp.cos(inner_angle)[:, None, :]
    sin_inner = jnp.sin(inner_angle)[:, None, :]
    wave_total = wave_order.shape[0]
    cosine = (cos_outer * cos_inner - sin_outer * sin_inner).reshape(wave_total, points)
    sines = (-(sin_outer * cos_inner + cos_outer * sin_inner)).reshape(wave_total, points)
    columns = jnp.arange(points, dtype=jnp.int32)
    alive = (wave_order[:, None] < live_count) & (columns[None, :] < cell_count)
    cosine = jnp.where(alive, cosine, jnp.zeros_like(cosine))
    sines = jnp.where(alive, sines, jnp.zeros_like(sines))
    return jnp.concatenate([cosine, sines], 0).astype(jnp.bfloat16)


def legendre_direct(lat_rows, legendre, owned):
    lat_total, level_depth, parts, slot_count = lat_rows.shape
    unpacked = lat_rows.reshape(lat_total, level_depth, parts, slot_count // 2, 2)
    results = jnp.einsum("qlrps,pcq->psrlc", unpacked, legendre, preferred_element_type=jnp.float32)
    return jnp.where(owned[:, None, None, :], results[:, 0], results[:, 1])


def shards(spec_in, legendre, wind, lat_weight, wave_order, lat_order, active):
    wide_count = lax.axis_size("wide")
    lev_count = lax.axis_size("lev")
    wide_pos = lax.axis_index("wide")
    lev_pos = lax.axis_index("lev")
    pairs_here, coef_count, lat_total = legendre.shape
    wave_total = coef_count - 1
    lat_here, levels, points = wind.shape
    level_depth = spec_in.shape[2]
    local_waves = lax.dynamic_slice_in_dim(wave_order, wide_pos * 2 * pairs_here, 2 * pairs_here)
    owned = (
        jnp.arange(coef_count, dtype=jnp.int32)[None, :] < (wave_total - local_waves[0::2])[:, None]
    )
    keep_mask = owned[:, None, None, :]
    nothing = jnp.zeros_like(spec_in)
    stacked = jnp.stack(
        [jnp.where(keep_mask, spec_in, nothing), jnp.where(keep_mask, nothing, spec_in)], 1
    )
    fourier = jnp.einsum(
        "psrlc,pcq->psrlq", stacked, legendre, preferred_element_type=jnp.float32
    ).astype(jnp.bfloat16)
    ordered = jnp.take(fourier, lat_order, axis=4)
    outgoing = jnp.transpose(ordered, (4, 3, 2, 0, 1)).reshape(
        lat_total, level_depth, 2, 2 * pairs_here
    )
    arrived = lax.all_to_all(
        lax.all_to_all(outgoing, "wide", split_axis=0, concat_axis=3, tiled=True),
        "lev",
        split_axis=0,
        concat_axis=1,
        tiled=True,
    )
    first_slot = (wide_pos * lev_count + lev_pos) * lat_here
    latitudes = lax.dynamic_slice_in_dim(lat_order, first_slot, lat_here)
    counts = jnp.take(active, latitudes)
    weights = jnp.take(lat_weight, latitudes)
    factors = jnp.where(wave_order == 0, 1.0, 2.0).astype(jnp.bfloat16)

    def per_lat(inputs):
        coeffs, wind_rows, live_count, weight = inputs
        basis_rows = make_basis(wave_order, live_count, points)
        scaled = (coeffs * factors).reshape(levels, 2 * wave_total)
        grid_rows = jnp.dot(scaled, basis_rows, preferred_element_type=jnp.float32).astype(
            jnp.bfloat16
        )
        product = (grid_rows.astype(jnp.float32) * wind_rows.astype(jnp.float32)).astype(
            jnp.bfloat16
        )
        folded = lax.dot_general(
            product, basis_rows, (((1,), (1,)), ((), ())), preferred_element_type=jnp.float32
        )
        folded = (folded * (weight / (4 * live_count).astype(jnp.float32))).astype(jnp.bfloat16)
        return (grid_rows, folded.reshape(levels, 2, wave_total))

    grid, folded = lax.map(per_lat, (arrived, wind, counts, weights))
    row_ids = jnp.arange(lat_total, dtype=jnp.int32)
    received = lax.all_to_all(
        lax.all_to_all(folded, "wide", split_axis=3, concat_axis=0, tiled=True),
        "lev",
        split_axis=1,
        concat_axis=0,
        tiled=True,
    )
    lev_src = row_ids // (wide_count * lat_here)
    wide_src = row_ids // lat_here % wide_count
    within = row_ids % lat_here
    slot_index = (wide_src * lev_count + lev_src) * lat_here + within
    position = jnp.zeros((lat_total,), jnp.int32).at[jnp.take(lat_order, slot_index)].set(row_ids)
    spec_out = legendre_direct(jnp.take(received, position, axis=0), legendre, owned)
    return (grid, spec_out)


def solution(mesh):
    in_specs = (
        P("wide", None, "lev", None),
        P("wide", None, None),
        P(("wide", "lev"), None, None),
        P(),
        P(),
        P(),
        P(),
    )
    out_specs = (P(("wide", "lev"), None, None), P("wide", None, "lev", None))
    return jax.shard_map(shards, mesh=mesh, in_specs=in_specs, out_specs=out_specs, check_vma=False)
```

profile of v0, /device:TPU:1, one launch (start us, length us, event | category | flops | bytes accessed | tf_op | source)
XLA Modules:
  0.0 220.1 jit_solution(6892341236998387838)
XLA Ops:
  3.8 4.6 %fusion.38 = bf16[5,2,2,1280]{3,2,1,0:T(2,128)(2,1)S(1)} fusion(bf16[5,641,1280]{2,1,0:T(8,128)(2,1)} %param.10, bf16[5,1,2,1,641]{4,2,1,0,3:T(2,128)(2,1)S(1)} %get-tuple-element.127, bf16[5,1,2,1,641]{4,2,1,0,3:T(2,128)(2,1)S(1)} %get-tuple-element.126), kind=kOutput, calls=%fused_computation.60 | convolution fusion | flops 32896080 | bytes 8281640 | tf_op jit(solution)/shard_map/psrlc,pcq->psrlq/dot_general | solution.py:57
  9.5 4.9 %gather_fusion = bf16[1280,5,2,2]{1,3,2,0:T(2,128)(2,1)S(1)} fusion(bf16[5,2,2,1280]{0,2,3,1:T(2,128)(2,1)S(1)} %copy.62, s32[2048]{0:T(1024)S(1)} %pad_clamp_fusion.2), kind=kCustom, calls=%fused_computation | custom fusion | bytes 107520 | tf_op jit(solution)/shard_map/jit(_take)/gather | solution.py:60
  14.4 4.7 %fusion.41 = bf16[1280,1,2,5,2]{3,2,4,0,1:T(2,128)(2,1)S(1)} fusion(bf16[1280,5,2,2]{1,3,2,0:T(2,128)(2,1)S(1)} %gather_fusion, pred[1280]{0:T(1024)(128)(4,1)S(1)} %compare_and_fusion.1), kind=kLoop, calls=%fused_computation.61 | loop fusion | flops 25600 | bytes 103680 | tf_op jit(solution)/shard_map/transpose | solution.py:61
  22.5 13.2 %all-to-all-start = ((bf16[64,2,200]{2,1,0:T(2,128)(2,1)}), bf16[64,2,200]{2,1,0:T(2,128)(2,1)S(1)}, u32[]{:S(2)}, u32[]{:S(2)}) async-start(bf16[64,2,200]{2,1,0:T(2,128)(2,1)} %reshape.446), calls=%async_computation | async-start | bytes 131072 | tf_op jit(solution)/shard_map/all_to_all | solution.py:65
  35.9 7.1 %gather_fusion.3 = s32[1280]{0:T(1024)S(1)} fusion(s32[1280]{0:T(1024)S(1)} %copy-done.1, s32[2048]{0:T(1024)S(1)} %pad_clamp_fusion.1), kind=kCustom, calls=%fused_computation.3 | custom fusion | bytes 15360 | tf_op jit(solution)/shard_map/jit(_take)/gather | solution.py:106
  43.1 5.2 %scatter_custom_fusion = s32[1280]{0:T(1024)S(1)} fusion(s32[1280]{0:T(1024)S(1)} %fusion.53, s32[1280]{0:T(1024)S(1)} %iota.38, s32[]{:T(128)} %constant.119.clone.1), kind=kCustom, calls=%fused_computation.105 | custom fusion | bytes 5124 | tf_op jit(solution)/shard_map/scatter | solution.py:106
  52.6 4.0 %all-to-all-start.1 = ((bf16[20,1,2,640]{3,2,1,0:T(2,128)(2,1)}), bf16[20,1,2,640]{3,2,1,0:T(2,128)(2,1)S(1)}, u32[]{:S(2)}, u32[]{:S(2)}) async-start(bf16[20,1,2,640]{3,2,1,0:T(2,128)(2,1)} %copy.67), calls=%async_computation.1 | async-start | bytes 102400 | tf_op jit(solution)/shard_map/all_to_all | solution.py:64
  56.7 4.3 %all-to-all-done.1 = bf16[20,1,2,640]{3,2,1,0:T(2,128)(2,1)S(1)} async-done(((bf16[20,1,2,640]{3,2,1,0:T(2,128)(2,1)}), bf16[20,1,2,640]{3,2,1,0:T(2,128)(2,1)S(1)}, u32[]{:S(2)}, u32[]{:S(2)}) %all-to-all-start.1) | async-done | bytes 51232 | tf_op jit(solution)/shard_map/all_to_all | solution.py:64
  61.0 105.5 %while.12 = (s32[]{:T(128)}, bf16[5,4,2560]{2,1,0:T(4,128)(2,1)S(1)}, bf16[5,4,2,640]{3,2,1,0:T(2,128)(2,1)S(1)}, bf16[5,4,2,640]{3,2,0,1:T(2,128)(2,1)S(1)}, bf...) while((s32[]{:T(128)}, ...), condition=%wide.region_1.2_spmd, body=%wide.region_0.1_spmd.sunk | while | flops 99431064 | bytes 34495892 | solution.py:93
  62.2 4.4 %fusion.67 = (f32[640,128]{0,1:T(8,128)S(1)}, f32[640,128]{0,1:T(8,128)S(1)}) fusion(f32[]{:T(128)S(6)} %convert_element_type.93, pred[]{:T(512)S(6)} %lt.253, s32[]{:T(128)S(6)} %select_n.357, s32[640]{0:T(1024)S(1)} %get-tuple-element.233), kind=kLoop, calls=%fused_computation.28.clone.1 | loop fusion | flops 901120 | bytes 657929 | tf_op jit(solution)/shard_map/while/body/eval_jaxpr/cos | solution.py:20
  74.0 3.9 %bitcast_dynamic-update-slice_fusion.2 = (bf16[5,4,2560]{2,1,0:T(4,128)(2,1)S(1)}, bf16[4,2560]{1,0:T(4,128)(2,1)}) fusion(bf16[5,4,2560]{2,1,0:T(4,128)(2,1)S(1)} %get-tuple-element.216, s32[]{:T(128)} %get-tuple-element.215, bf16[640,2560]{0,1:T(8,128)(2,1)} %get-tuple-element.199, bf16[640,2560]{0,1:T(8,128)(2,1)S(1)} %get-tuple-element.200, ...), kind=kOutput, calls=%fused_computation.43.clone.1 | convolution fusion | flops 39352320 | bytes 6608900 | tf_op jit(solution)/shard_map/while/body/eval_jaxpr/dot_general | solution.py:81
  83.3 4.4 %fusion.67 = (f32[640,128]{0,1:T(8,128)S(1)}, f32[640,128]{0,1:T(8,128)S(1)}) fusion(f32[]{:T(128)S(6)} %convert_element_type.93, pred[]{:T(512)S(6)} %lt.253, s32[]{:T(128)S(6)} %select_n.357, s32[640]{0:T(1024)S(1)} %get-tuple-element.233), kind=kLoop, calls=%fused_computation.28.clone.1 | loop fusion | flops 901120 | bytes 657929 | tf_op jit(solution)/shard_map/while/body/eval_jaxpr/cos | solution.py:20
  95.1 3.9 %bitcast_dynamic-update-slice_fusion.2 = (bf16[5,4,2560]{2,1,0:T(4,128)(2,1)S(1)}, bf16[4,2560]{1,0:T(4,128)(2,1)}) fusion(bf16[5,4,2560]{2,1,0:T(4,128)(2,1)S(1)} %get-tuple-element.216, s32[]{:T(128)} %get-tuple-element.215, bf16[640,2560]{0,1:T(8,128)(2,1)} %get-tuple-element.199, bf16[640,2560]{0,1:T(8,128)(2,1)S(1)} %get-tuple-element.200, ...), kind=kOutput, calls=%fused_computation.43.clone.1 | convolution fusion | flops 39352320 | bytes 6608900 | tf_op jit(solution)/shard_map/while/body/eval_jaxpr/dot_general | solution.py:81
  104.4 4.4 %fusion.67 = (f32[640,128]{0,1:T(8,128)S(1)}, f32[640,128]{0,1:T(8,128)S(1)}) fusion(f32[]{:T(128)S(6)} %convert_element_type.93, pred[]{:T(512)S(6)} %lt.253, s32[]{:T(128)S(6)} %select_n.357, s32[640]{0:T(1024)S(1)} %get-tuple-element.233), kind=kLoop, calls=%fused_computation.28.clone.1 | loop fusion | flops 901120 | bytes 657929 | tf_op jit(solution)/shard_map/while/body/eval_jaxpr/cos | solution.py:20
  125.5 4.4 %fusion.67 = (f32[640,128]{0,1:T(8,128)S(1)}, f32[640,128]{0,1:T(8,128)S(1)}) fusion(f32[]{:T(128)S(6)} %convert_element_type.93, pred[]{:T(512)S(6)} %lt.253, s32[]{:T(128)S(6)} %select_n.357, s32[640]{0:T(1024)S(1)} %get-tuple-element.233), kind=kLoop, calls=%fused_computation.28.clone.1 | loop fusion | flops 901120 | bytes 657929 | tf_op jit(solution)/shard_map/while/body/eval_jaxpr/cos | solution.py:20
  137.3 3.9 %bitcast_dynamic-update-slice_fusion.2 = (bf16[5,4,2560]{2,1,0:T(4,128)(2,1)S(1)}, bf16[4,2560]{1,0:T(4,128)(2,1)}) fusion(bf16[5,4,2560]{2,1,0:T(4,128)(2,1)S(1)} %get-tuple-element.216, s32[]{:T(128)} %get-tuple-element.215, bf16[640,2560]{0,1:T(8,128)(2,1)} %get-tuple-element.199, bf16[640,2560]{0,1:T(8,128)(2,1)S(1)} %get-tuple-element.200, ...), kind=kOutput, calls=%fused_computation.43.clone.1 | convolution fusion | flops 39352320 | bytes 6608900 | tf_op jit(solution)/shard_map/while/body/eval_jaxpr/dot_general | solution.py:81
  146.6 4.4 %fusion.67 = (f32[640,128]{0,1:T(8,128)S(1)}, f32[640,128]{0,1:T(8,128)S(1)}) fusion(f32[]{:T(128)S(6)} %convert_element_type.93, pred[]{:T(512)S(6)} %lt.253, s32[]{:T(128)S(6)} %select_n.357, s32[640]{0:T(1024)S(1)} %get-tuple-element.233), kind=kLoop, calls=%fused_computation.28.clone.1 | loop fusion | flops 901120 | bytes 657929 | tf_op jit(solution)/shard_map/while/body/eval_jaxpr/cos | solution.py:20
  158.4 3.9 %bitcast_dynamic-update-slice_fusion.2 = (bf16[5,4,2560]{2,1,0:T(4,128)(2,1)S(1)}, bf16[4,2560]{1,0:T(4,128)(2,1)}) fusion(bf16[5,4,2560]{2,1,0:T(4,128)(2,1)S(1)} %get-tuple-element.216, s32[]{:T(128)} %get-tuple-element.215, bf16[640,2560]{0,1:T(8,128)(2,1)} %get-tuple-element.199, bf16[640,2560]{0,1:T(8,128)(2,1)S(1)} %get-tuple-element.200, ...), kind=kOutput, calls=%fused_computation.43.clone.1 | convolution fusion | flops 39352320 | bytes 6608900 | tf_op jit(solution)/shard_map/while/body/eval_jaxpr/dot_general | solution.py:81
  170.3 11.7 %all-to-all-start.2 = ((bf16[64,2,200]{2,1,0:T(2,128)(2,1)}), bf16[64,2,200]{2,1,0:T(2,128)(2,1)S(1)}, u32[]{:S(2)}, u32[]{:S(2)}) async-start(bf16[64,2,200]{2,1,0:T(2,128)(2,1)} %reshape.448), calls=%async_computation.2 | async-start | bytes 131072 | tf_op jit(solution)/shard_map/all_to_all | solution.py:96
  182.0 10.1 %all-to-all-done.2 = bf16[64,2,200]{2,1,0:T(2,128)(2,1)S(1)} async-done(((bf16[64,2,200]{2,1,0:T(2,128)(2,1)}), bf16[64,2,200]{2,1,0:T(2,128)(2,1)S(1)}, u32[]{:S(2)}, u32[]{:S(2)}) %all-to-all-start.2) | async-done | bytes 51232 | tf_op jit(solution)/shard_map/all_to_all | solution.py:96
  193.0 5.7 %copy.80 = bf16[5,4,2,64,10]{4,3,2,1,0:T(8,128)(2,1)S(1)} copy(bf16[5,4,2,64,10]{0,1,2,4,3:T(4,128)(2,1)S(1)} %bitcast.99) | data formatting | bytes 102400 | tf_op jit(solution)/shard_map/all_to_all | solution.py:96
  203.9 4.4 %all-to-all-done.3 = bf16[320,4,2,10]{0,2,3,1:T(2,128)(2,1)S(1)} async-done(((bf16[320,4,2,10]{0,2,3,1:T(2,128)(2,1)}), bf16[320,4,2,10]{0,2,3,1:T(2,128)(2,1)S(1)}, u32[]{:S(2)}, u32[]{:S(2)}) %all-to-all-start.3) | async-done | bytes 51232 | tf_op jit(solution)/shard_map/all_to_all | solution.py:95
  208.9 4.4 %gather_fusion.4 = bf16[1280,2,10]{2,1,0:T(2,128)(2,1)S(1)} fusion(bf16[1280,2,10]{2,1,0:T(2,128)(2,1)S(1)} %bitcast.100, s32[2048]{0:T(1024)S(1)} %pad_clamp_fusion), kind=kCustom, calls=%fused_computation.4 | custom fusion | bytes 107520 | tf_op jit(solution)/shard_map/jit(_take)/gather | solution.py:107
  213.8 5.6 %fusion.42 = f32[5,2,2,1,641]{4,2,0,3,1:T(2,128)S(1)} fusion(bf16[5,641,1280]{2,1,0:T(8,128)(2,1)} %param.10, bf16[1280,2,5,2]{0,1,3,2:T(2,128)(2,1)S(1)} %bitcast.107, pred[1280]{0:T(1024)(128)(4,1)S(1)} %compare_and_fusion), kind=kOutput, calls=%fused_computation.62 | convolution fusion | flops 32844800 | bytes 8308560 | tf_op jit(solution)/shard_map/qlrps,pcq->psrlc/dot_general | solution.py:35
  (129 shorter events, 85.0 us)
Async XLA Ops:
  0.6 47.7 %copy-start = (f32[1280]{0:T(1024)S(1)}, f32[1280]{0:T(1024)}, u32[]{:S(2)}) copy-start(f32[1280]{0:T(1024)} %param.12) | copy-start | bytes 15364
  3.8 31.9 %copy-start.3 = (s32[640]{0:T(1024)S(1)}, s32[640]{0:T(1024)}, u32[]{:S(2)}) copy-start(s32[640]{0:T(1024)} %param.13) | copy-start | bytes 7684
  3.8 32.0 %copy-start.1 = (s32[1280]{0:T(1024)S(1)}, s32[1280]{0:T(1024)}, u32[]{:S(2)}) copy-start(s32[1280]{0:T(1024)} %param.14) | copy-start | bytes 15364
  19.1 30.0 %copy-start.2 = (s32[1280]{0:T(1024)S(1)}, s32[1280]{0:T(1024)}, u32[]{:S(2)}) copy-start(s32[1280]{0:T(1024)} %param.15) | copy-start | bytes 15364
  22.5 27.2 %all-to-all-start = ((bf16[64,2,200]{2,1,0:T(2,128)(2,1)}), bf16[64,2,200]{2,1,0:T(2,128)(2,1)S(1)}, u32[]{:S(2)}, u32[]{:S(2)}) async-start(bf16[64,2,200]{2,1,0:T(2,128)(2,1)} %reshape.446), calls=%async_computation | async-start | bytes 131072 | tf_op jit(solution)/shard_map/all_to_all | solution.py:65
  52.6 8.4 %all-to-all-start.1 = ((bf16[20,1,2,640]{3,2,1,0:T(2,128)(2,1)}), bf16[20,1,2,640]{3,2,1,0:T(2,128)(2,1)S(1)}, u32[]{:S(2)}, u32[]{:S(2)}) async-start(bf16[20,1,2,640]{3,2,1,0:T(2,128)(2,1)} %copy.67), calls=%async_computation.1 | async-start | bytes 102400 | tf_op jit(solution)/shard_map/all_to_all | solution.py:64
  166.5 52.9 %copy-start.4 = (bf16[5,4,2560]{2,1,0:T(4,128)(2,1)}, bf16[5,4,2560]{2,1,0:T(4,128)(2,1)S(1)}, u32[]{:S(2)}) copy-start(bf16[5,4,2560]{2,1,0:T(4,128)(2,1)S(1)} %get-tuple-element.96) | copy-start | bytes 307204
  170.3 21.8 %all-to-all-start.2 = ((bf16[64,2,200]{2,1,0:T(2,128)(2,1)}), bf16[64,2,200]{2,1,0:T(2,128)(2,1)S(1)}, u32[]{:S(2)}, u32[]{:S(2)}) async-start(bf16[64,2,200]{2,1,0:T(2,128)(2,1)} %reshape.448), calls=%async_computation.2 | async-start | bytes 131072 | tf_op jit(solution)/shard_map/all_to_all | solution.py:96
  200.6 7.7 %all-to-all-start.3 = ((bf16[320,4,2,10]{0,2,3,1:T(2,128)(2,1)}), bf16[320,4,2,10]{0,2,3,1:T(2,128)(2,1)S(1)}, u32[]{:S(2)}, u32[]{:S(2)}) async-start(bf16[320,4,2,10]{0,2,3,1:T(2,128)(2,1)} %copy.72), calls=%async_computation.3 | async-start | bytes 122880 | tf_op jit(solution)/shard_map/all_to_all | solution.py:95
where the time goes:
time: 221 us; the launch traced here: 220 us
  other arithmetic  65.8 us (30%)
  local copies, waits for them, and re-layouts  51.2 us (23%)
  matrix products  44.2 us (20%)
  starting transfers between devices  32.2 us (15%)
  waiting for transfers between devices  18.8 us (9%)
  loops' own time  6.96 us (3%)
    cos x5, other arithmetic, make_basis(): cos_inner = jnp.cos(inner_angle)[:, None, :]  21.8 us
    dot_general x5, matrix products, per_lat(): jnp.dot(scaled, basis_rows, preferred_element_type=jnp.float32)  19.4 us
    another operation x5, other arithmetic  16.4 us
    dot_general x5, matrix products, per_lat(): lax.dot_general(product, basis_rows, (((1,), (1,)), ((), ())), preferred_...  14.6 us
    all_to_all x1, starting transfers between devices, shards(): lax.all_to_all(outgoing, 'wide', split_axis=0, concat_axis=3, tiled=True)  13.2 us
    sub x5, other arithmetic, make_basis(): cos_outer * cos_inner - sin_outer * sin_inner  12.1 us
    all_to_all x1, starting transfers between devices, shards(): lax.all_to_all(folded, 'wide', split_axis=3, concat_axis=0, tiled=True)  11.7 us
    all_to_all x1, waiting for transfers between devices, shards(): lax.all_to_all(folded, 'wide', split_axis=3, concat_axis=0, tiled=True)  10.1 us
  transfers between devices with their start and end apart: 4, of which 3 were waited for; matrix products, arithmetic and copies ran while one was open for 6% of the time, Pallas kernels for 0%

commit v1 on v0

--- a/solution.py
+++ b/solution.py
@@ -61,12 +61,20 @@
     outgoing = jnp.transpose(ordered, (4, 3, 2, 0, 1)).reshape(
         lat_total, level_depth, 2, 2 * pairs_here
     )
-    arrived = lax.all_to_all(
-        lax.all_to_all(outgoing, "wide", split_axis=0, concat_axis=3, tiled=True),
-        "lev",
-        split_axis=0,
-        concat_axis=1,
-        tiled=True,
+    arrived = jnp.concatenate(
+        lax.all_to_all(
+            jnp.stack(
+                jnp.split(
+                    lax.all_to_all(outgoing, "wide", split_axis=0, concat_axis=3, tiled=True),
+                    lax.axis_size("lev"),
+                    axis=0,
+                )
+            ),
+            "lev",
+            0,
+            0,
+        ),
+        axis=1,
     )
     first_slot = (wide_pos * lev_count + lev_pos) * lat_here
     latitudes = lax.dynamic_slice_in_dim(lat_order, first_slot, lat_here)

time: 221 us -> 227 us (1.027)
  local copies, waits for them, and re-layouts: 51.2 us -> 55.9 us
    split x0 -> x5, local copies, waits for them, and re-layouts: none -> 4.61 us  [shards(): jnp.split(lax.all_to_all(outgoing, 'wide', split_axis=0, concat_axis=3, t...]
    another operation x5 -> x6, other arithmetic: 16.4 us -> 17.1 us
where the time goes in v1:
time: 227 us; the launch traced here: 226 us
  other arithmetic  66.6 us (29%)
  local copies, waits for them, and re-layouts  55.9 us (25%)
  matrix products  44.2 us (19%)
  starting transfers between devices  32.2 us (14%)
  waiting for transfers between devices  18.8 us (8%)
  loops' own time  6.96 us (3%)
    cos x5, other arithmetic, make_basis(): cos_inner = jnp.cos(inner_angle)[:, None, :]  21.8 us
    dot_general x5, matrix products, per_lat(): jnp.dot(scaled, basis_rows, preferred_element_type=jnp.float32)  19.4 us
    another operation x5, other arithmetic  16.4 us
    dot_general x5, matrix products, per_lat(): lax.dot_general(product, basis_rows, (((1,), (1,)), ((), ())), preferred_...  14.6 us
    all_to_all x1, starting transfers between devices, shards(): lax.all_to_all(outgoing, 'wide', split_axis=0, concat_axis=3, tiled=True)  13.2 us
    sub x5, other arithmetic, make_basis(): cos_outer * cos_inner - sin_outer * sin_inner  12.2 us
    all_to_all x1, starting transfers between devices, shards(): lax.all_to_all(folded, 'wide', split_axis=3, concat_axis=0, tiled=True)  11.7 us
    all_to_all x1, waiting for transfers between devices, shards(): lax.all_to_all(folded, 'wide', split_axis=3, concat_axis=0, tiled=True)  10.1 us
  transfers between devices with their start and end apart: 4, of which 3 were waited for; matrix products, arithmetic and copies ran while one was open for 6% of the time, Pallas kernels for 0%

profile of v1, /device:TPU:1, one launch (start us, length us, event | category | flops | bytes accessed | tf_op | source)
XLA Modules:
  0.0 225.7 jit_solution(4414157471503090915)
XLA Ops:
  3.8 4.6 %fusion.38 = bf16[5,2,2,1280]{3,2,1,0:T(2,128)(2,1)S(1)} fusion(bf16[5,641,1280]{2,1,0:T(8,128)(2,1)} %param.10, bf16[5,1,2,1,641]{4,2,1,0,3:T(2,128)(2,1)S(1)} %get-tuple-element.131, bf16[5,1,2,1,641]{4,2,1,0,3:T(2,128)(2,1)S(1)} %get-tuple-element.130), kind=kOutput, calls=%fused_computation.60 | convolution fusion | flops 32896080 | bytes 8281640 | tf_op jit(solution)/shard_map/psrlc,pcq->psrlq/dot_general | solution.py:57
  9.5 4.9 %gather_fusion = bf16[1280,5,2,2]{1,3,2,0:T(2,128)(2,1)S(1)} fusion(bf16[5,2,2,1280]{0,2,3,1:T(2,128)(2,1)S(1)} %copy.69, s32[2048]{0:T(1024)S(1)} %pad_clamp_fusion.2), kind=kCustom, calls=%fused_computation | custom fusion | bytes 107520 | tf_op jit(solution)/shard_map/jit(_take)/gather | solution.py:60
  14.4 4.7 %fusion.41 = bf16[1280,1,2,5,2]{3,2,4,0,1:T(2,128)(2,1)S(1)} fusion(bf16[1280,5,2,2]{1,3,2,0:T(2,128)(2,1)S(1)} %gather_fusion, pred[1280]{0:T(1024)(128)(4,1)S(1)} %compare_and_fusion.1), kind=kLoop, calls=%fused_computation.61 | loop fusion | flops 25600 | bytes 103680 | tf_op jit(solution)/shard_map/transpose | solution.py:61
  22.5 13.2 %all-to-all-start = ((bf16[64,2,200]{2,1,0:T(2,128)(2,1)}), bf16[64,2,200]{2,1,0:T(2,128)(2,1)S(1)}, u32[]{:S(2)}, u32[]{:S(2)}) async-start(bf16[64,2,200]{2,1,0:T(2,128)(2,1)} %reshape.462), calls=%async_computation | async-start | bytes 131072 | tf_op jit(solution)/shard_map/all_to_all | solution.py:68
  35.9 7.1 %gather_fusion.3 = s32[1280]{0:T(1024)S(1)} fusion(s32[1280]{0:T(1024)S(1)} %copy-done.1, s32[2048]{0:T(1024)S(1)} %pad_clamp_fusion.1), kind=kCustom, calls=%fused_computation.3 | custom fusion | bytes 15360 | tf_op jit(solution)/shard_map/jit(_take)/gather | solution.py:114
  43.0 5.4 %scatter_custom_fusion = s32[1280]{0:T(1024)S(1)} fusion(s32[1280]{0:T(1024)S(1)} %fusion.53, s32[1280]{0:T(1024)S(1)} %iota.38, s32[]{:T(128)} %constant.119.clone.1), kind=kCustom, calls=%fused_computation.106 | custom fusion | bytes 5124 | tf_op jit(solution)/shard_map/scatter | solution.py:114
  58.0 4.0 %all-to-all-start.1 = ((bf16[4,5,1,2,640]{4,3,1,2,0:T(2,128)(2,1)}), bf16[4,5,1,2,640]{4,3,1,2,0:T(2,128)(2,1)S(1)}, u32[]{:S(2)}, u32[]{:S(2)}) async-start(bf16[4,5,1,2,640]{4,3,1,2,0:T(2,128)(2,1)} %pad_maximum_fusion.9), calls=%async_computation.1 | async-start | bytes 102400 | tf_op jit(solution)/shard_map/all_to_all | solution.py:65
  62.1 4.3 %all-to-all-done.1 = bf16[4,5,1,2,640]{4,3,1,2,0:T(2,128)(2,1)S(1)} async-done(((bf16[4,5,1,2,640]{4,3,1,2,0:T(2,128)(2,1)}), bf16[4,5,1,2,640]{4,3,1,2,0:T(2,128)(2,1)S(1)}, u32[]{:S(2)}, u32[]{:S(2)}) %all-to-all-start.1) | async-done | bytes 51232 | tf_op jit(solution)/shard_map/all_to_all | solution.py:65
  66.4 105.5 %while.12 = (s32[]{:T(128)}, bf16[5,4,2560]{2,1,0:T(4,128)(2,1)S(1)}, bf16[5,4,2,640]{3,2,1,0:T(2,128)(2,1)S(1)}, bf16[5,4,2,640]{3,2,0,1:T(2,128)(2,1)S(1)}, bf...) while((s32[]{:T(128)}, ...), condition=%wide.region_1.2_spmd, body=%wide.region_0.1_spmd.sunk | while | flops 99431064 | bytes 34495892 | solution.py:101
  67.7 4.4 %fusion.68 = (f32[640,128]{0,1:T(8,128)S(1)}, f32[640,128]{0,1:T(8,128)S(1)}) fusion(f32[]{:T(128)S(6)} %convert_element_type.93, pred[]{:T(512)S(6)} %lt.253, s32[]{:T(128)S(6)} %select_n.357, s32[640]{0:T(1024)S(1)} %get-tuple-element.237), kind=kLoop, calls=%fused_computation.28.clone.1 | loop fusion | flops 901120 | bytes 657929 | tf_op jit(solution)/shard_map/while/body/eval_jaxpr/cos | solution.py:20
  79.5 3.9 %bitcast_dynamic-update-slice_fusion.2 = (bf16[5,4,2560]{2,1,0:T(4,128)(2,1)S(1)}, bf16[4,2560]{1,0:T(4,128)(2,1)}) fusion(bf16[5,4,2560]{2,1,0:T(4,128)(2,1)S(1)} %get-tuple-element.220, s32[]{:T(128)} %get-tuple-element.219, bf16[640,2560]{0,1:T(8,128)(2,1)} %get-tuple-element.203, bf16[640,2560]{0,1:T(8,128)(2,1)S(1)} %get-tuple-element.204, ...), kind=kOutput, calls=%fused_computation.43.clone.1 | convolution fusion | flops 39352320 | bytes 6608900 | tf_op jit(solution)/shard_map/while/body/eval_jaxpr/dot_general | solution.py:89
  88.8 4.4 %fusion.68 = (f32[640,128]{0,1:T(8,128)S(1)}, f32[640,128]{0,1:T(8,128)S(1)}) fusion(f32[]{:T(128)S(6)} %convert_element_type.93, pred[]{:T(512)S(6)} %lt.253, s32[]{:T(128)S(6)} %select_n.357, s32[640]{0:T(1024)S(1)} %get-tuple-element.237), kind=kLoop, calls=%fused_computation.28.clone.1 | loop fusion | flops 901120 | bytes 657929 | tf_op jit(solution)/shard_map/while/body/eval_jaxpr/cos | solution.py:20
  100.6 3.9 %bitcast_dynamic-update-slice_fusion.2 = (bf16[5,4,2560]{2,1,0:T(4,128)(2,1)S(1)}, bf16[4,2560]{1,0:T(4,128)(2,1)}) fusion(bf16[5,4,2560]{2,1,0:T(4,128)(2,1)S(1)} %get-tuple-element.220, s32[]{:T(128)} %get-tuple-element.219, bf16[640,2560]{0,1:T(8,128)(2,1)} %get-tuple-element.203, bf16[640,2560]{0,1:T(8,128)(2,1)S(1)} %get-tuple-element.204, ...), kind=kOutput, calls=%fused_computation.43.clone.1 | convolution fusion | flops 39352320 | bytes 6608900 | tf_op jit(solution)/shard_map/while/body/eval_jaxpr/dot_general | solution.py:89
  109.9 4.4 %fusion.68 = (f32[640,128]{0,1:T(8,128)S(1)}, f32[640,128]{0,1:T(8,128)S(1)}) fusion(f32[]{:T(128)S(6)} %convert_element_type.93, pred[]{:T(512)S(6)} %lt.253, s32[]{:T(128)S(6)} %select_n.357, s32[640]{0:T(1024)S(1)} %get-tuple-element.237), kind=kLoop, calls=%fused_computation.28.clone.1 | loop fusion | flops 901120 | bytes 657929 | tf_op jit(solution)/shard_map/while/body/eval_jaxpr/cos | solution.py:20
  121.7 3.9 %bitcast_dynamic-update-slice_fusion.2 = (bf16[5,4,2560]{2,1,0:T(4,128)(2,1)S(1)}, bf16[4,2560]{1,0:T(4,128)(2,1)}) fusion(bf16[5,4,2560]{2,1,0:T(4,128)(2,1)S(1)} %get-tuple-element.220, s32[]{:T(128)} %get-tuple-element.219, bf16[640,2560]{0,1:T(8,128)(2,1)} %get-tuple-element.203, bf16[640,2560]{0,1:T(8,128)(2,1)S(1)} %get-tuple-element.204, ...), kind=kOutput, calls=%fused_computation.43.clone.1 | convolution fusion | flops 39352320 | bytes 6608900 | tf_op jit(solution)/shard_map/while/body/eval_jaxpr/dot_general | solution.py:89
  131.0 4.4 %fusion.68 = (f32[640,128]{0,1:T(8,128)S(1)}, f32[640,128]{0,1:T(8,128)S(1)}) fusion(f32[]{:T(128)S(6)} %convert_element_type.93, pred[]{:T(512)S(6)} %lt.253, s32[]{:T(128)S(6)} %select_n.357, s32[640]{0:T(1024)S(1)} %get-tuple-element.237), kind=kLoop, calls=%fused_computation.28.clone.1 | loop fusion | flops 901120 | bytes 657929 | tf_op jit(solution)/shard_map/while/body/eval_jaxpr/cos | solution.py:20
  152.1 4.4 %fusion.68 = (f32[640,128]{0,1:T(8,128)S(1)}, f32[640,128]{0,1:T(8,128)S(1)}) fusion(f32[]{:T(128)S(6)} %convert_element_type.93, pred[]{:T(512)S(6)} %lt.253, s32[]{:T(128)S(6)} %select_n.357, s32[640]{0:T(1024)S(1)} %get-tuple-element.237), kind=kLoop, calls=%fused_computation.28.clone.1 | loop fusion | flops 901120 | bytes 657929 | tf_op jit(solution)/shard_map/while/body/eval_jaxpr/cos | solution.py:20
  163.9 3.9 %bitcast_dynamic-update-slice_fusion.2 = (bf16[5,4,2560]{2,1,0:T(4,128)(2,1)S(1)}, bf16[4,2560]{1,0:T(4,128)(2,1)}) fusion(bf16[5,4,2560]{2,1,0:T(4,128)(2,1)S(1)} %get-tuple-element.220, s32[]{:T(128)} %get-tuple-element.219, bf16[640,2560]{0,1:T(8,128)(2,1)} %get-tuple-element.203, bf16[640,2560]{0,1:T(8,128)(2,1)S(1)} %get-tuple-element.204, ...), kind=kOutput, calls=%fused_computation.43.clone.1 | convolution fusion | flops 39352320 | bytes 6608900 | tf_op jit(solution)/shard_map/while/body/eval_jaxpr/dot_general | solution.py:89
  175.8 11.7 %all-to-all-start.2 = ((bf16[64,2,200]{2,1,0:T(2,128)(2,1)}), bf16[64,2,200]{2,1,0:T(2,128)(2,1)S(1)}, u32[]{:S(2)}, u32[]{:S(2)}) async-start(bf16[64,2,200]{2,1,0:T(2,128)(2,1)} %reshape.464), calls=%async_computation.2 | async-start | bytes 131072 | tf_op jit(solution)/shard_map/all_to_all | solution.py:104
  187.6 10.1 %all-to-all-done.2 = bf16[64,2,200]{2,1,0:T(2,128)(2,1)S(1)} async-done(((bf16[64,2,200]{2,1,0:T(2,128)(2,1)}), bf16[64,2,200]{2,1,0:T(2,128)(2,1)S(1)}, u32[]{:S(2)}, u32[]{:S(2)}) %all-to-all-start.2) | async-done | bytes 51232 | tf_op jit(solution)/shard_map/all_to_all | solution.py:104
  198.5 5.7 %copy.89 = bf16[5,4,2,64,10]{4,3,2,1,0:T(8,128)(2,1)S(1)} copy(bf16[5,4,2,64,10]{0,1,2,4,3:T(4,128)(2,1)S(1)} %bitcast.113) | data formatting | bytes 102400 | tf_op jit(solution)/shard_map/all_to_all | solution.py:104
  209.5 4.4 %all-to-all-done.3 = bf16[320,4,2,10]{0,2,3,1:T(2,128)(2,1)S(1)} async-done(((bf16[320,4,2,10]{0,2,3,1:T(2,128)(2,1)}), bf16[320,4,2,10]{0,2,3,1:T(2,128)(2,1)S(1)}, u32[]{:S(2)}, u32[]{:S(2)}) %all-to-all-start.3) | async-done | bytes 51232 | tf_op jit(solution)/shard_map/all_to_all | solution.py:103
  214.4 4.4 %gather_fusion.4 = bf16[1280,2,10]{2,1,0:T(2,128)(2,1)S(1)} fusion(bf16[1280,2,10]{2,1,0:T(2,128)(2,1)S(1)} %bitcast.114, s32[2048]{0:T(1024)S(1)} %pad_clamp_fusion), kind=kCustom, calls=%fused_computation.4 | custom fusion | bytes 107520 | tf_op jit(solution)/shard_map/jit(_take)/gather | solution.py:115
  219.4 5.6 %fusion.42 = f32[5,2,2,1,641]{4,2,0,3,1:T(2,128)S(1)} fusion(bf16[5,641,1280]{2,1,0:T(8,128)(2,1)} %param.10, bf16[1280,2,5,2]{0,1,3,2:T(2,128)(2,1)S(1)} %bitcast.119, pred[1280]{0:T(1024)(128)(4,1)S(1)} %compare_and_fusion), kind=kOutput, calls=%fused_computation.62 | convolution fusion | flops 32844800 | bytes 8308560 | tf_op jit(solution)/shard_map/qlrps,pcq->psrlc/dot_general | solution.py:35
  (137 shorter events, 90.3 us)
Async XLA Ops:
  0.6 47.9 %copy-start = (f32[1280]{0:T(1024)S(1)}, f32[1280]{0:T(1024)}, u32[]{:S(2)}) copy-start(f32[1280]{0:T(1024)} %param.12) | copy-start | bytes 15364
  3.8 31.9 %copy-start.3 = (s32[640]{0:T(1024)S(1)}, s32[640]{0:T(1024)}, u32[]{:S(2)}) copy-start(s32[640]{0:T(1024)} %param.13) | copy-start | bytes 7684
  3.8 32.0 %copy-start.1 = (s32[1280]{0:T(1024)S(1)}, s32[1280]{0:T(1024)}, u32[]{:S(2)}) copy-start(s32[1280]{0:T(1024)} %param.14) | copy-start | bytes 15364
  19.1 30.1 %copy-start.2 = (s32[1280]{0:T(1024)S(1)}, s32[1280]{0:T(1024)}, u32[]{:S(2)}) copy-start(s32[1280]{0:T(1024)} %param.15) | copy-start | bytes 15364
  22.5 27.4 %all-to-all-start = ((bf16[64,2,200]{2,1,0:T(2,128)(2,1)}), bf16[64,2,200]{2,1,0:T(2,128)(2,1)S(1)}, u32[]{:S(2)}, u32[]{:S(2)}) async-start(bf16[64,2,200]{2,1,0:T(2,128)(2,1)} %reshape.462), calls=%async_computation | async-start | bytes 131072 | tf_op jit(solution)/shard_map/all_to_all | solution.py:68
  58.0 8.4 %all-to-all-start.1 = ((bf16[4,5,1,2,640]{4,3,1,2,0:T(2,128)(2,1)}), bf16[4,5,1,2,640]{4,3,1,2,0:T(2,128)(2,1)S(1)}, u32[]{:S(2)}, u32[]{:S(2)}) async-start(bf16[4,5,1,2,640]{4,3,1,2,0:T(2,128)(2,1)} %pad_maximum_fusion.9), calls=%async_computation.1 | async-start | bytes 102400 | tf_op jit(solution)/shard_map/all_to_all | solution.py:65
  172.0 53.0 %copy-start.4 = (bf16[5,4,2560]{2,1,0:T(4,128)(2,1)}, bf16[5,4,2560]{2,1,0:T(4,128)(2,1)S(1)}, u32[]{:S(2)}) copy-start(bf16[5,4,2560]{2,1,0:T(4,128)(2,1)S(1)} %get-tuple-element.96) | copy-start | bytes 307204
  175.8 21.8 %all-to-all-start.2 = ((bf16[64,2,200]{2,1,0:T(2,128)(2,1)}), bf16[64,2,200]{2,1,0:T(2,128)(2,1)S(1)}, u32[]{:S(2)}, u32[]{:S(2)}) async-start(bf16[64,2,200]{2,1,0:T(2,128)(2,1)} %reshape.464), calls=%async_computation.2 | async-start | bytes 131072 | tf_op jit(solution)/shard_map/all_to_all | solution.py:104
  206.2 7.7 %all-to-all-start.3 = ((bf16[320,4,2,10]{0,2,3,1:T(2,128)(2,1)}), bf16[320,4,2,10]{0,2,3,1:T(2,128)(2,1)S(1)}, u32[]{:S(2)}, u32[]{:S(2)}) async-start(bf16[320,4,2,10]{0,2,3,1:T(2,128)(2,1)} %copy.81), calls=%async_computation.3 | async-start | bytes 122880 | tf_op jit(solution)/shard_map/all_to_all | solution.py:103
